TPU v7x, 32 devices: a whole 2x2x4 slice. The times are simulated.
32 devices in a mesh: row: 8 (over z, y), col: 4 (over x, core).
Axes of the slice: x: 2, y: 2, z: 4, core: 2. Of those that a mesh axis runs over, the one named last changes fastest.
Arguments:
- queries: bfloat16 [1024, 1024], P('row', 'col'), may hold values from -26 to 26
- key_vectors: bfloat16 [1024, 1024], P('row', 'col'), may hold values from -8 to 8
- values: bfloat16 [1024, 1024], P('row', 'col'), may hold values from -6 to 6
- sink_logit: float32 [8], P('col'), may hold values from -1 to 5
- lengths: int32 [8], replicated, may hold values from 1 to 576, as said below
- stream: bfloat16 [1024, 2048], P('row', 'col'), may hold values from -60 to 60
- out_weight: bfloat16 [1024, 2048], P('col', 'row'), may hold values from -0.1875 to 0.1875
- norm_gain: bfloat16 [2048], P('col'), may hold values from 0.25 to 1.75
- shared_gate: bfloat16 [2048, 2816], P('row', 'col'), may hold values from -0.125 to 0.125
- shared_up: bfloat16 [2048, 2816], P('row', 'col'), may hold values from -0.125 to 0.125
- shared_down: bfloat16 [2816, 2048], P('col', 'row'), may hold values from -0.109375 to 0.109375
- shared_switch: bfloat16 [2048], replicated, may hold values from -0.125 to 0.125
- expert_gate: bfloat16 [8, 2048, 1408], P('row', None, 'col'), may hold values from -0.125 to 0.125
- expert_up: bfloat16 [8, 2048, 1408], P('row', None, 'col'), may hold values from -0.125 to 0.125
- expert_down: bfloat16 [8, 1408, 2048], P('row', 'col'), may hold values from -0.15625 to 0.15625
- routes: int32 [1024, 4], P('row'), may hold values from 0 to 7, all different within a row; in each aligned block of 128 rows (0 to 127, 128 to 255, ...) at most 96 rows name the same one
- route_weights: float32 [1024, 4], P('row'), may hold values from 0.05 to 0.6
Outputs:
- attended: bfloat16 [1024, 1024], P('row', 'col')
- layer_out: bfloat16 [1024, 2048], P('row', 'col')
Inputs may be any that keep to these rules, and one draw needn't show every extreme that they name: `routes`: each row names 4 different experts; among the 128 rows of one device (aligned blocks) no expert is named more than 96 times, a bound that some block reaches. The lengths sum to 1024; exactly one prompt has 576 tokens.
All inputs are finite; a program needn't handle non-finite values.
Results may differ from a plain program's by a relative error of at most 0.01.
Values may be sent and summed in bfloat16 or wider, within the bound.
A program may use at most 128 MiB of HBM per device.

v0:
```python
import math

import jax
import jax.numpy as jnp
from jax import lax
from jax.sharding import PartitionSpec as P

HDIM = 128
WINDOW = 4096


norm_eps = 1e-06
masked_score = -1e30


def lower_bounds(lengths, positions):
    doc_ends = jnp.cumsum(lengths)
    starts = doc_ends - lengths
    begun_docs = starts[None, :] <= positions[:, None]
    doc_start = jnp.max(jnp.where(begun_docs, starts[None, :], 0), axis=1)
    return jnp.maximum(doc_start, positions - WINDOW + 1)


def body(
    queries,
    key_vectors,
    values,
    sink_logit,
    lengths,
    stream,
    out_weight,
    norm_gain,
    shared_gate,
    shared_up,
    shared_down,
    shared_switch,
    expert_gate,
    expert_up,
    expert_down,
    routes,
    route_weights,
):
    local_tokens = queries.shape[0]
    feature_width = queries.shape[1]
    head_count = feature_width // HDIM
    my_row = lax.axis_index("row")
    positions = my_row * local_tokens + jnp.arange(local_tokens, dtype=jnp.int32)
    lower_bound = lower_bounds(lengths, positions)
    query_heads = queries.reshape(local_tokens, head_count, HDIM)
    score_scale = 1.0 / math.sqrt(HDIM)
    key_value = jnp.stack([key_vectors, values], 0)
    key_piece = lax.all_gather(key_value, "row", axis=1, tiled=True)
    row_max = jnp.broadcast_to(sink_logit[None, :], (local_tokens, head_count))
    denominator = jnp.ones((local_tokens, head_count), jnp.float32)
    numerator = jnp.zeros((local_tokens, head_count, HDIM), jnp.float32)
    needed = key_piece.shape[1]
    key_heads = key_piece[0].reshape(needed, head_count, HDIM)
    value_heads = key_piece[1].reshape(needed, head_count, HDIM)
    scores = (
        jnp.einsum("qhd,khd->qhk", query_heads, key_heads, preferred_element_type=jnp.float32)
        * score_scale
    )
    key_places = jnp.arange(needed, dtype=jnp.int32)
    visible = (
        (key_places[None, :] >= lower_bound[:, None]) & (key_places[None, :] <= positions[:, None])
    )[:, None, :]
    masked = jnp.where(visible, scores, masked_score)
    new_max = jnp.maximum(row_max, jnp.max(masked, axis=2))
    weight = jnp.where(visible, jnp.exp(masked - new_max[:, :, None]), 0.0)
    rescale = jnp.exp(row_max - new_max)
    denominator = denominator * rescale + jnp.sum(weight, axis=2)
    numerator = numerator * rescale[:, :, None] + jnp.einsum(
        "qhk,khd->qhd", weight.astype(jnp.bfloat16), value_heads, preferred_element_type=jnp.float32
    )
    final_max, denominator, numerator = (new_max, denominator, numerator)
    attended = (
        (numerator / denominator[:, :, None])
        .reshape(local_tokens, feature_width)
        .astype(jnp.bfloat16)
    )
    head_terms = jnp.dot(
        attended,
        lax.all_gather(out_weight, "row", axis=1, tiled=True),
        preferred_element_type=jnp.float32,
    )
    mixed_heads = lax.psum_scatter(
        head_terms.astype(jnp.bfloat16), "col", scatter_dimension=1, tiled=True
    ).astype(jnp.float32)
    hidden = (stream.astype(jnp.float32) + mixed_heads).astype(jnp.bfloat16)
    widened = hidden.astype(jnp.float32)
    full_width = lax.axis_size("col") * hidden.shape[1]
    squares = lax.psum(jnp.sum(widened * widened, axis=1), "col")
    row_scale = lax.rsqrt(squares / full_width + norm_eps)
    normed_part = (widened * row_scale[:, None] * norm_gain.astype(jnp.float32)).astype(
        jnp.bfloat16
    )
    normed = lax.all_gather(normed_part, "col", axis=1, tiled=True)
    gate_part = jnp.dot(
        normed,
        lax.all_gather(shared_gate, "row", axis=0, tiled=True),
        preferred_element_type=jnp.float32,
    )
    up_part = jnp.dot(
        normed,
        lax.all_gather(shared_up, "row", axis=0, tiled=True),
        preferred_element_type=jnp.float32,
    )
    shared_act = (jax.nn.silu(gate_part) * up_part).astype(jnp.bfloat16)
    shared_part = jnp.dot(
        shared_act,
        lax.all_gather(shared_down, "row", axis=1, tiled=True),
        preferred_element_type=jnp.float32,
    )
    switch = jax.nn.sigmoid(jnp.dot(normed, shared_switch, preferred_element_type=jnp.float32))
    row_count = lax.axis_size("row")
    fanout = routes.shape[1]
    model_width = normed.shape[1]
    capacity = max(2, min(local_tokens, 3 * local_tokens * fanout // (2 * row_count)))
    flat_routes = routes.reshape(-1)
    onehot = (flat_routes[:, None] == jnp.arange(row_count, dtype=jnp.int32)[None, :]).astype(
        jnp.int32
    )
    before = jnp.cumsum(onehot, axis=0) - onehot
    slot_index = jnp.sum(before * onehot, axis=1)
    target = flat_routes * capacity + slot_index
    owner_row = jnp.arange(local_tokens * fanout, dtype=jnp.int32) // fanout
    source = jnp.full((row_count * capacity,), local_tokens, jnp.int32).at[target].set(owner_row)
    padded = jnp.concatenate([normed, jnp.zeros((1, model_width), jnp.bfloat16)], 0)
    outgoing = padded[source].reshape(row_count, capacity, model_width)
    received = lax.all_to_all(outgoing, "row", split_axis=0, concat_axis=0, tiled=True)
    senders, slot_count, received_width = received.shape
    dispatched = received.reshape(senders * slot_count, received_width)
    gate_out = jnp.dot(dispatched, expert_gate[0], preferred_element_type=jnp.float32)
    up_out = jnp.dot(dispatched, expert_up[0], preferred_element_type=jnp.float32)
    activation = (jax.nn.silu(gate_out) * up_out).astype(jnp.bfloat16)
    partial_out = jnp.dot(activation, expert_down[0], preferred_element_type=jnp.float32).astype(
        jnp.bfloat16
    )
    returned = lax.all_to_all(
        partial_out.reshape(senders, slot_count, received_width),
        "row",
        split_axis=0,
        concat_axis=0,
        tiled=True,
    )
    route_rows = returned.reshape(row_count * capacity, model_width)[target].reshape(
        local_tokens, fanout, model_width
    )
    routed = jnp.zeros((local_tokens, model_width), jnp.float32)
    for route_slot in range(fanout):
        routed = routed + route_weights[:, route_slot][:, None] * route_rows[
            :, route_slot, :
        ].astype(jnp.float32)
    layer_terms = switch[:, None] * shared_part + routed
    summed = lax.psum_scatter(
        layer_terms.astype(jnp.bfloat16), "col", scatter_dimension=1, tiled=True
    ).astype(jnp.float32)
    layer_out = (hidden.astype(jnp.float32) + summed).astype(jnp.bfloat16)
    return (attended, layer_out)


def solution(mesh):
    return jax.shard_map(
        body,
        mesh=mesh,
        in_specs=(
            P("row", "col"),
            P("row", "col"),
            P("row", "col"),
            P("col"),
            P(),
            P("row", "col"),
            P("col", "row"),
            P("col"),
            P("row", "col"),
            P("row", "col"),
            P("col", "row"),
            P(),
            P("row", None, "col"),
            P("row", None, "col"),
            P("row", "col", None),
            P("row", None),
            P("row", None),
        ),
        out_specs=(P("row", "col"), P("row", "col")),
        check_vma=False,
    )
```

profile of v0, /device:TPU:0, one launch (start us, length us, event | category | flops | bytes accessed | tf_op | source)
XLA Modules:
  0.0 430.8 jit_solution(6506192966484894538)
XLA Ops:
  7.2 0.0 copy-start
  7.2 0.0 all-gather.6.cloned.1.call-start
  7.2 1.1 copy.36
  8.3 1.0 copy.37
  9.3 0.7 pad_maximum_fusion
  9.9 0.0 all-gather.6.cloned.1.call-update
  10.0 0.0 copy-start.10
  10.0 0.0 all-gather.8.cloned.1.call-start
  10.0 0.7 all-gather.8.cloned.1.call-update
  10.7 0.0 reduce-scatter.3.cloned.1.call-start
  10.8 0.8 reduce-window.19
  11.6 0.7 bitcast_subtract_fusion.1
  12.3 0.1 select_reduce_fusion
  12.4 0.1 fusion.34
  12.5 40.4 %all-gather.6.cloned.1.call-done = bf16[2,1024,256]{1,2,0:T(8,128)(2,1)} async-done(((bf16[2,128,256]{1,2,0:T(8,128)(2,1)}), bf16[2,1024,256]{1,2,0:T(8,128)(2,1)}) %all-gather.6.cloned.1.call-update) | async-done | bytes 1048592 | tf_op jit(solution)/shard_map/all_gather | solution.py:52
  52.9 1.3 fusion.62
  54.2 0.4 fusion.63
  54.6 0.1 broadcast_maximum_fusion
  54.6 0.2 fusion.28
  54.9 0.1 fusion.57
  55.0 0.4 fusion.18
  55.4 38.0 %all-gather.8.cloned.1.call-done = bf16[256,2048]{1,0:T(8,128)(2,1)} async-done(((bf16[256,256]{1,0:T(8,128)(2,1)}), bf16[256,2048]{1,0:T(8,128)(2,1)}) %all-gather.8.cloned.1.call-update) | async-done | bytes 1048592 | tf_op jit(solution)/shard_map/all_gather | solution.py:83
  93.4 2.4 convolution_convert_fusion.1
  95.8 0.0 reduce-scatter.3.cloned.1.call-update
  95.8 0.0 all-gather.10.cloned.1.call-start
  95.9 0.5 all-gather.10.cloned.1.call-update
  96.4 0.1 copy.42
  96.5 0.1 eq.29
  96.6 0.1 eq.25
  96.8 1.1 reduce-window.20
  97.9 0.2 slice_reduce_fusion
  98.2 0.1 copy.41
  98.3 0.1 mul.135
  98.4 0.1 fusion.49
  98.5 2.4 scatter_custom_fusion
  101.0 15.5 %reduce-scatter.3.cloned.1.call-done = bf16[128,512]{1,0:T(8,128)(2,1)} async-done(((bf16[128,2048]{1,0:T(8,128)(2,1)}), bf16[128,512]{1,0:T(8,128)(2,1)}) %reduce-scatter.3.cloned.1.call-update) | async-done | bytes 131088 | tf_op jit(solution)/shard_map/reduce_scatter | solution.py:86
  116.5 1.0 fusion.41
  117.5 5.8 %psum.7 = f32[128]{0:T(128)S(1)} all-reduce(f32[128]{0:T(128)S(1)} %fusion.41), channel_id=1, replica_groups=mesh['row'=8,'col'=4] {'col'}, use_global_device_ids=true, to_apply=%region_6.7 | all-reduce | flops 128 | bytes 1024 | tf_op jit(solution)/shard_map/psum | solution.py:92
  123.3 1.0 fusion.43
  124.3 7.3 %all_gather.20 = bf16[128,2048]{1,0:T(8,128)(2,1)S(1)} all-gather(bf16[128,512]{1,0:T(8,128)(2,1)S(1)} %fusion.43), channel_id=1, replica_groups=mesh['row'=8,'col'=4] {'col'}, dimensions={1}, use_global_device_ids=true | all-gather | bytes 655360 | tf_op jit(solution)/shard_map/all_gather | solution.py:97
  131.7 4.3 gather_fusion
  135.9 5.5 %all-to-all-start = ((bf16[8,96,2048]{2,1,0:T(8,128)(2,1)}), bf16[8,96,2048]{2,1,0:T(8,128)(2,1)}, u32[]{:S(2)}, u32[]{:S(2)}) async-start(bf16[8,96,2048]{2,1,0:T(8,128)(2,1)} %bitcast.109), calls=%async_computation.1 | async-start | bytes 6291456 | tf_op jit(solution)/shard_map/all_to_all | solution.py:130
  141.5 0.0 all-gather.12.cloned.1.call-start
  141.5 0.5 all-gather.12.cloned.1.call-update
  142.1 94.2 %all-to-all-done = bf16[8,96,2048]{2,1,0:T(8,128)(2,1)} async-done(((bf16[8,96,2048]{2,1,0:T(8,128)(2,1)}), bf16[8,96,2048]{2,1,0:T(8,128)(2,1)}, u32[]{:S(2)}, u32[]{:S(2)}) %all-to-all-start) | async-done | bytes 3145760 | tf_op jit(solution)/shard_map/all_to_all | solution.py:130
  236.2 4.7 %fusion.5 = f32[768,352]{0,1:T(8,128)} fusion(bf16[768,2048]{1,0:T(8,128)(2,1)} %bitcast.16, bf16[1,2048,352]{1,2,0:T(8,128)(2,1)} %param.29), kind=kOutput, calls=%fused_computation.11 | convolution fusion | flops 1107296256 | bytes 5668864 | tf_op jit(solution)/shard_map/dot_general | solution.py:133
  240.9 8.0 %convolution_convert_fusion = bf16[768,2048]{1,0:T(8,128)(2,1)} fusion(bf16[1,352,2048]{2,1,0:T(8,128)(2,1)S(1)} %copy-done, bf16[768,2048]{1,0:T(8,128)(2,1)} %bitcast.16, bf16[1,2048,352]{1,2,0:T(8,128)(2,1)} %param.30, f32[768,352]{0,1:T(8,128)} %fusion.5), kind=kOutput, calls=%fused_computation.3 | convolution fusion | flops 2217787392 | bytes 10256384 | tf_op jit(solution)/shard_map/dot_general | solution.py:136
  248.9 4.6 %all-to-all-start.1 = ((bf16[8,96,2048]{2,1,0:T(8,128)(2,1)}), bf16[8,96,2048]{2,1,0:T(8,128)(2,1)}, u32[]{:S(2)}, u32[]{:S(2)}) async-start(bf16[8,96,2048]{2,1,0:T(8,128)(2,1)} %bitcast.110), calls=%async_computation.2 | async-start | bytes 6291456 | tf_op jit(solution)/shard_map/all_to_all | solution.py:139
  253.5 0.0 all-gather.14.cloned.1.call-start
  253.6 0.5 all-gather.14.cloned.1.call-update
  254.1 0.2 reduce-scatter.5.cloned.1.call-start
  254.4 0.5 slice_bitcast_fusion.3
  254.9 0.3 fusion.22
  255.1 3.5 fusion.64
  258.6 92.9 %all-to-all-done.1 = bf16[8,96,2048]{2,1,0:T(8,128)(2,1)} async-done(((bf16[8,96,2048]{2,1,0:T(8,128)(2,1)}), bf16[8,96,2048]{2,1,0:T(8,128)(2,1)}, u32[]{:S(2)}, u32[]{:S(2)}) %all-to-all-start.1) | async-done | bytes 3145760 | tf_op jit(solution)/shard_map/all_to_all | solution.py:139
  351.5 7.5 %gather_fusion.1 = bf16[512,2048]{1,0:T(8,128)(2,1)} fusion(bf16[768,2048]{1,0:T(8,128)(2,1)} %bitcast.21, s32[1024]{0:T(1024)S(1)} %pad_clamp_fusion), kind=kCustom, calls=%fused_computation.1 | custom fusion | bytes 4196352 | tf_op jit(solution)/shard_map/gather | solution.py:146
  359.0 2.7 reshape.220
  361.8 4.5 %fusion.61 = (bf16[128,1,2048]{2,1,0:T(2,128)(2,1)}, bf16[128,1,2048]{2,1,0:T(2,128)(2,1)}, bf16[128,1,2048]{2,1,0:T(2,128)(2,1)}, bf16[128,1,2048]{2,1,0:T(2,128)(2,1)}) fusion(bf16[128,4,2048]{2,1,0:T(4,128)(2,1)S(1)} %reshape.220), kind=kLoop, calls=%fused_computation.104 | loop fusion | bytes 4194304 | tf_op jit(solution)/shard_map/slice | solution.py:151
  366.3 27.9 %all-gather.14.cloned.1.call-done = bf16[704,2048]{1,0:T(8,128)(2,1)} async-done(((bf16[704,256]{1,0:T(8,128)(2,1)}), bf16[704,2048]{1,0:T(8,128)(2,1)}) %all-gather.14.cloned.1.call-update) | async-done | bytes 2883600 | tf_op jit(solution)/shard_map/all_gather | solution.py:111
  394.2 8.1 %fusion.1 = bf16[128,2048]{1,0:T(8,128)(2,1)} fusion(bf16[704,2048]{1,0:T(8,128)(2,1)} %all-gather.14.cloned.1.call-done, bf16[128,2048]{1,0:T(8,128)(2,1)} %copy-done.1, bf16[2048,704]{0,1:T(8,128)(2,1)} %all-gather.12.cloned.1.call-done, bf16[128,1,2048]{2,1,0:T(2,128)(2,1)} %get-tuple-element.11, bf16[128,1,2048]{2,1,0:T(2,128)(2,1)} %get-tuple-element.9, ...), kind=kOutput, calls=%fused_computation.6 | convolution fusion | flops 742408192 | bytes 9275904 | tf_op jit(solution)/shard_map/dot_general | solution.py:109
  402.3 0.0 reduce-scatter.5.cloned.1.call-update
  402.3 0.7 copy.48
  403.1 19.3 %reduce-scatter.5.cloned.1.call-done = bf16[128,512]{1,0:T(8,128)(2,1)} async-done(((bf16[128,2048]{1,0:T(8,128)(2,1)}), bf16[128,512]{1,0:T(8,128)(2,1)}) %reduce-scatter.5.cloned.1.call-update) | async-done | bytes 131088 | tf_op jit(solution)/shard_map/reduce_scatter | solution.py:155
  422.3 1.6 fusion.44
  (41 shorter events, 0.2 us)
Async XLA Ops:
  7.2 233.7 %copy-start = (bf16[1,352,2048]{2,1,0:T(8,128)(2,1)S(1)}, bf16[1,352,2048]{2,1,0:T(8,128)(2,1)}, u32[]{:S(2)}) copy-start(bf16[1,352,2048]{2,1,0:T(8,128)(2,1)} %param.31) | copy-start | bytes 4325380
  7.2 47.0 %copy-start.7 = (bf16[128,256]{1,0:T(8,128)(2,1)S(1)}, bf16[128,256]{1,0:T(8,128)(2,1)}, u32[]{:S(2)}) copy-start(bf16[128,256]{1,0:T(8,128)(2,1)} %param.17) | copy-start | bytes 196612
  7.2 45.7 %all-gather.6.cloned.1.call-start = ((), (), s32[]{:S(2)}) async-start(), calls=%async_computation.4 | async-start | bytes 1179648 | tf_op jit(solution)/shard_map/all_gather | solution.py:52
  10.0 44.6 %copy-start.10 = (f32[2]{0:T(128)S(1)}, f32[2]{0:T(128)}, u32[]{:S(2)}) copy-start(f32[2]{0:T(128)} %param.20) | copy-start | bytes 28
  10.0 83.4 %all-gather.8.cloned.1.call-start = ((), (), s32[]{:S(2)}) async-start(), calls=%async_computation.5 | async-start | bytes 1179648 | tf_op jit(solution)/shard_map/all_gather | solution.py:83
  10.7 105.8 %reduce-scatter.3.cloned.1.call-start = ((), (), s32[]{:S(2)}) async-start(), calls=%async_computation.6 | async-start | bytes 655360 | tf_op jit(solution)/shard_map/reduce_scatter | solution.py:86
  54.9 41.4 %copy-start.8 = (s32[128,4]{0,1:T(4,128)S(1)}, s32[128,4]{0,1:T(4,128)}, u32[]{:S(2)}) copy-start(s32[128,4]{0,1:T(4,128)} %param.32) | copy-start | bytes 6148
  54.9 41.8 %copy-start.12 = (bf16[512]{0:T(512)(128)(2,1)S(1)}, bf16[512]{0:T(512)(128)(2,1)}, u32[]{:S(2)}) copy-start(bf16[512]{0:T(512)(128)(2,1)} %param.24) | copy-start | bytes 3076
  55.3 40.5 %copy-start.5 = (bf16[128,2,128]{0,2,1:T(8,128)(2,1)}, bf16[128,2,128]{0,2,1:T(8,128)(2,1)S(1)}, u32[]{:S(2)}) copy-start(bf16[128,2,128]{0,2,1:T(8,128)(2,1)S(1)} %fusion.18) | copy-start | bytes 196612
  55.4 61.1 %copy-start.2 = (bf16[128,512]{1,0:T(8,128)(2,1)S(1)}, bf16[128,512]{1,0:T(8,128)(2,1)}, u32[]{:S(2)}) copy-start(bf16[128,512]{1,0:T(8,128)(2,1)} %param.22) | copy-start | bytes 393220
  95.8 159.3 %all-gather.10.cloned.1.call-start = ((), (), s32[]{:S(2)}) async-start(), calls=%async_computation.7 | async-start | bytes 3244032 | tf_op jit(solution)/shard_map/all_gather | solution.py:100
  131.6 123.5 %copy-start.1 = (bf16[128,2048]{1,0:T(8,128)(2,1)}, bf16[128,2048]{1,0:T(8,128)(2,1)S(1)}, u32[]{:S(2)}) copy-start(bf16[128,2048]{1,0:T(8,128)(2,1)S(1)} %all_gather.20) | copy-start | bytes 1572868
  135.9 100.3 %all-to-all-start = ((bf16[8,96,2048]{2,1,0:T(8,128)(2,1)}), bf16[8,96,2048]{2,1,0:T(8,128)(2,1)}, u32[]{:S(2)}, u32[]{:S(2)}) async-start(bf16[8,96,2048]{2,1,0:T(8,128)(2,1)} %bitcast.109), calls=%async_computation.1 | async-start | bytes 6291456 | tf_op jit(solution)/shard_map/all_to_all | solution.py:130
  141.5 224.8 %all-gather.12.cloned.1.call-start = ((), (), s32[]{:S(2)}) async-start(), calls=%async_computation.8 | async-start | bytes 3244032 | tf_op jit(solution)/shard_map/all_gather | solution.py:105
  248.9 5.4 %copy-start.9 = (bf16[2048]{0:T(1024)(128)(2,1)S(1)}, bf16[2048]{0:T(1024)(128)(2,1)}, u32[]{:S(2)}) copy-start(bf16[2048]{0:T(1024)(128)(2,1)} %param.28) | copy-start | bytes 12292
  248.9 5.4 %copy-start.11 = (f32[128,4]{0,1:T(4,128)S(1)}, f32[128,4]{0,1:T(4,128)}, u32[]{:S(2)}) copy-start(f32[128,4]{0,1:T(4,128)} %param.33) | copy-start | bytes 6148
  248.9 102.6 %all-to-all-start.1 = ((bf16[8,96,2048]{2,1,0:T(8,128)(2,1)}), bf16[8,96,2048]{2,1,0:T(8,128)(2,1)}, u32[]{:S(2)}, u32[]{:S(2)}) async-start(bf16[8,96,2048]{2,1,0:T(8,128)(2,1)} %bitcast.110), calls=%async_computation.2 | async-start | bytes 6291456 | tf_op jit(solution)/shard_map/all_to_all | solution.py:139
  253.5 140.7 %all-gather.14.cloned.1.call-start = ((), (), s32[]{:S(2)}) async-start(), calls=%async_computation.9 | async-start | bytes 3244032 | tf_op jit(solution)/shard_map/all_gather | solution.py:111
  254.1 168.3 %reduce-scatter.5.cloned.1.call-start = ((), (), s32[]{:S(2)}) async-start(), calls=%async_computation.10 | async-start | bytes 655360 | tf_op jit(solution)/shard_map/reduce_scatter | solution.py:155
  394.2 8.1 %copy-start.6 = (bf16[128,2,128]{0,2,1:T(8,128)(2,1)S(1)}, bf16[128,2,128]{0,2,1:T(8,128)(2,1)}, u32[]{:S(2)}) copy-start(bf16[128,2,128]{0,2,1:T(8,128)(2,1)} %copy-done.5) | copy-start | bytes 196612
  394.2 28.1 %copy-start.3 = (bf16[128,512]{1,0:T(8,128)(2,1)S(1)}, bf16[128,512]{1,0:T(8,128)(2,1)}, u32[]{:S(2)}) copy-start(bf16[128,512]{1,0:T(8,128)(2,1)} %param.22) | copy-start | bytes 393220
  394.2 28.1 %copy-start.4 = (bf16[128,512]{1,0:T(8,128)(2,1)S(1)}, bf16[128,512]{1,0:T(8,128)(2,1)}, u32[]{:S(2)}) copy-start(bf16[128,512]{1,0:T(8,128)(2,1)} %reduce-scatter.3.cloned.1.call-done) | copy-start | bytes 393220
Sparse Core Ops, SparseCore 0:
  10.6 42.2 all-gather.5
  55.0 38.4 all-gather.7
  95.9 20.5 reduce-scatter.2
  118.6 109.6 all-gather.9
  230.3 102.7 all-gather.11
  335.3 58.9 all-gather.13
  402.4 19.8 reduce-scatter.4
where the time goes:
time: 431 us
  waiting for transfers between devices  330 us (77%)
  matrix products  27.7 us (6%)
  local copies, waits for them, and re-layouts  26.9 us (6%)
  between operations  14.4 us (3%)
  blocking collectives  13.1 us (3%)
  starting transfers between devices  10.6 us (2%)
  other arithmetic  7.72 us (2%)
    all_to_all x1, waiting for transfers between devices, body(): lax.all_to_all(outgoing, 'row', split_axis=0, concat_axis=0, tiled=True)  94.2 us
    all_to_all x1, waiting for transfers between devices, body(): lax.all_to_all(partial_out.reshape(senders, slot_count, received_width),...  92.9 us
    all_gather x1, waiting for transfers between devices, body(): key_piece = lax.all_gather(key_value, 'row', axis=1, tiled=True)  40.4 us
    all_gather x1, waiting for transfers between devices, body(): lax.all_gather(out_weight, 'row', axis=1, tiled=True)  38 us
    all_gather x1, waiting for transfers between devices, body(): lax.all_gather(shared_down, 'row', axis=1, tiled=True)  27.9 us
    reduce_scatter x1, waiting for transfers between devices, body(): lax.psum_scatter(layer_terms.astype(jnp.bfloat16), 'col', scatter_dimensi...  19.3 us
    reduce_scatter x1, waiting for transfers between devices, body(): lax.psum_scatter(head_terms.astype(jnp.bfloat16), 'col', scatter_dimensio...  15.5 us
  transfers between devices with their start and end apart: 9, of which 7 were waited for; matrix products, arithmetic and copies ran while one was open for 11% of the time, Pallas kernels for 0%

commit v1 on v0

--- a/solution.py
+++ b/solution.py
@@ -3,6 +3,8 @@
 import jax
 import jax.numpy as jnp
 from jax import lax
+from jax.experimental import pallas as pl
+from jax.experimental.pallas import tpu as pltpu
 from jax.sharding import PartitionSpec as P
 
 HDIM = 128
@@ -21,7 +23,459 @@
     return jnp.maximum(doc_start, positions - WINDOW + 1)
 
 
-def body(
+MESH = pl.DeviceIdType.MESH
+LONGEST = 576
+ROWS = 8
+COLS = 4
+TOK = 128
+WIDTH = 2048
+PART = WIDTH // COLS
+SLICE = WIDTH // ROWS
+UNITS = 96
+REACH = (LONGEST - 2 + TOK) // TOK
+NT = (((1,), (1,)), ((), ()))
+
+
+def mm(a, b):
+    return jnp.dot(a, b, preferred_element_type=jnp.float32)
+
+
+def layer_kernel(
+    q_ref,
+    k_ref,
+    v_ref,
+    sink_ref,
+    lower_ref,
+    stream_ref,
+    wo_ref,
+    gain_ref,
+    sh_ref,
+    switch_ref,
+    eg_ref,
+    eu_ref,
+    ed_ref,
+    w_ref,
+    att_ref,
+    out_ref,
+    kv_buf,
+    wo_buf,
+    gain_buf,
+    sh_buf,
+    w_buf,
+    head_send,
+    head_recv,
+    hid,
+    own_hidden,
+    keep_a,
+    keep_b,
+    send1,
+    recv1,
+    send2,
+    recv2,
+    send3,
+    recv3,
+    s_kv,
+    r_kv,
+    s_wo,
+    r_wo,
+    s_gain,
+    r_gain,
+    s_sh,
+    r_sh,
+    s_w,
+    r_w,
+    s_head,
+    r_head,
+    s_row,
+    r_row,
+    s_core,
+    r_core,
+    s_x,
+    r_x,
+    s_fwd,
+    r_fwd,
+    s_1,
+    r_1,
+    s_2,
+    r_2,
+    s_3,
+    r_3,
+):
+    r = lax.axis_index("row")
+    c = lax.axis_index("col")
+    core_peer = c + 1 - 2 * (c % 2)
+    x_peer = (c + 2) % COLS
+    far_peer = (core_peer + 2) % COLS
+
+    def up(k):
+        return (r + k) % ROWS
+
+    def down(k):
+        return (r + ROWS - k) % ROWS
+
+    def cols(i, n):
+        return pl.ds(pl.multiple_of(i * n, n), n)
+
+    barrier = pltpu.get_barrier_semaphore()
+    for k in range(1, ROWS):
+        pl.semaphore_signal(barrier, inc=1, device_id=(up(k), c), device_id_type=MESH)
+    for k in range(1, COLS):
+        pl.semaphore_signal(barrier, inc=1, device_id=(r, (c + k) % COLS), device_id_type=MESH)
+    pl.semaphore_wait(barrier, ROWS - 1 + COLS - 1)
+
+    def push(src, dst, send, recv, where):
+        return pltpu.make_async_remote_copy(
+            src_ref=src,
+            dst_ref=dst,
+            send_sem=send,
+            recv_sem=recv,
+            device_id=where,
+            device_id_type=MESH,
+        )
+
+    def k_copy(k):
+        return push(
+            k_ref, kv_buf.at[0, pl.ds(k * TOK, TOK)], s_kv.at[0, k], r_kv.at[0, k], (up(k), c)
+        )
+
+    def v_copy(k):
+        return push(
+            v_ref, kv_buf.at[1, pl.ds(k * TOK, TOK)], s_kv.at[1, k], r_kv.at[1, k], (up(k), c)
+        )
+
+    def wo_copy(k, block):
+        return push(wo_ref, wo_buf.at[:, cols(block, SLICE)], s_wo.at[k], r_wo.at[k], (up(k), c))
+
+    def sh_copy(k, block):
+        return push(
+            sh_ref.at[up(k)],
+            sh_buf.at[:, :, cols(block, SLICE)],
+            s_sh.at[k],
+            r_sh.at[k],
+            (up(k), c),
+        )
+
+    def w_copy(k):
+        return push(w_ref.at[up(k)], w_buf.at[k], s_w.at[k], r_w.at[k], (up(k), c))
+
+    def gain_copy(k, block):
+        return push(
+            gain_ref,
+            gain_buf.at[:, cols(block, PART)],
+            s_gain.at[k],
+            r_gain.at[k],
+            (r, (c + k) % COLS),
+        )
+
+    def head_copy(k):
+        return push(
+            head_send.at[k], head_recv.at[k], s_head.at[k], r_head.at[k], (r, (c + k) % COLS)
+        )
+
+    for k in range(1, REACH + 1):
+
+        @pl.when(r + k < ROWS)
+        def _():
+            k_copy(k).start()
+            v_copy(k).start()
+
+    for k in range(1, ROWS):
+        wo_copy(k, r).start()
+    for k in range(1, COLS):
+        gain_copy(k, c).start()
+    for k in range(1, ROWS):
+        w_copy(k).start()
+    for k in range(1, ROWS):
+        sh_copy(k, r).start()
+
+    kv_buf[0, 0:TOK] = k_ref[...]
+    kv_buf[1, 0:TOK] = v_ref[...]
+    wo_buf[:, cols(r, SLICE)] = wo_ref[...]
+    gain_buf[:, cols(c, PART)] = gain_ref[...]
+    sh_buf[:, :, cols(r, SLICE)] = sh_ref[r]
+    w_buf[0] = w_ref[r]
+
+    for k in range(1, REACH + 1):
+
+        @pl.when(r >= k)
+        def _():
+            k_copy(k).wait_recv()
+            v_copy(k).wait_recv()
+
+        @pl.when(r < k)
+        def _():
+            kv_buf[:, k * TOK : (k + 1) * TOK] = jnp.zeros((2, TOK, 2 * HDIM), jnp.bfloat16)
+
+    keys = (REACH + 1) * TOK
+    place = lax.broadcasted_iota(jnp.int32, (TOK, keys), 1)
+    key_place = (r - place // TOK) * TOK + place % TOK
+    positions = r * TOK + lax.broadcasted_iota(jnp.int32, (TOK, keys), 0)
+    visible = (key_place >= lower_ref[...]) & (key_place <= positions)
+    for h in range(2):
+        lanes = slice(h * HDIM, (h + 1) * HDIM)
+        scores = lax.dot_general(
+            q_ref[:, lanes], kv_buf[0, :, lanes], NT, preferred_element_type=jnp.float32
+        ) * (1.0 / math.sqrt(HDIM))
+        masked = jnp.where(visible, scores, masked_score)
+        sink = sink_ref[0:1, h * HDIM : h * HDIM + 1]
+        row_max = jnp.maximum(jnp.max(masked, axis=1, keepdims=True), sink)
+        weight = jnp.where(visible, jnp.exp(masked - row_max), 0.0)
+        denominator = jnp.exp(sink - row_max) + jnp.sum(weight, axis=1, keepdims=True)
+        mixture = mm(weight.astype(jnp.bfloat16), kv_buf[1, :, lanes])
+        att_ref[:, lanes] = (mixture / denominator).astype(jnp.bfloat16)
+
+    for k in range(1, ROWS):
+        wo_copy(k, down(k)).wait_recv()
+    attended = att_ref[...]
+    for k in range(1, COLS):
+        head_send[k] = mm(attended, wo_buf[:, cols((c + k) % COLS, PART)]).astype(jnp.bfloat16)
+        head_copy(k).start()
+    total = stream_ref[...].astype(jnp.float32) + mm(attended, wo_buf[:, cols(c, PART)])
+    for k in range(1, COLS):
+        head_copy(k).wait_recv()
+        total = total + head_recv[k].astype(jnp.float32)
+    hidden = total.astype(jnp.bfloat16)
+    own_hidden[...] = hidden
+    hid[cols(r, TOK), cols(c, PART)] = hidden
+
+    def row_copy(k, block):
+        return push(
+            own_hidden,
+            hid.at[cols(block, TOK), cols(c, PART)],
+            s_row.at[k],
+            r_row.at[k],
+            (up(k), c),
+        )
+
+    def side_copy(k, col, send, recv, peer):
+        piece = hid.at[cols(down(k), TOK), cols(col, PART)]
+        return push(piece, piece, send.at[k], recv.at[k], (r, peer))
+
+    def copy1(k):
+        return push(send1.at[k], recv1.at[k], s_1.at[k], r_1.at[k], (r, core_peer))
+
+    def copy2(k):
+        return push(send2.at[k], recv2.at[k], s_2.at[k], r_2.at[k], (r, x_peer))
+
+    def copy3(k):
+        return push(send3.at[k], recv3.at[k], s_3.at[k], r_3.at[k], (down(k), c))
+
+    for k in range(1, ROWS):
+        row_copy(k, r).start()
+
+    for k in range(1, ROWS):
+        sh_copy(k, down(k)).wait_recv()
+        w_copy(k).wait_recv()
+    for k in range(1, COLS):
+        gain_copy(k, (c + COLS - k) % COLS).wait_recv()
+
+    def experts(k):
+        widened = hid[cols(down(k), TOK), :].astype(jnp.float32)
+        mean = jnp.mean(widened * widened, axis=1, keepdims=True)
+        normed = (widened * lax.rsqrt(mean + norm_eps) * gain_buf[0:1, :]).astype(jnp.bfloat16)
+        logit = jnp.sum(
+            normed.astype(jnp.float32) * switch_ref[...].astype(jnp.float32), axis=1, keepdims=True
+        )
+        switch = 1.0 / (1.0 + jnp.exp(-logit))
+        weights = jnp.broadcast_to(w_buf[k, 0:1, :], (TOK, TOK)).T[:, 0:1]
+        gate = mm(normed, eg_ref[...])
+        act = gate / (1.0 + jnp.exp(-gate)) * mm(normed, eu_ref[...])
+        act = (act * weights).astype(jnp.bfloat16)
+        gate = lax.dot_general(normed, sh_buf[0], NT, preferred_element_type=jnp.float32)
+        raised = lax.dot_general(normed, sh_buf[1], NT, preferred_element_type=jnp.float32)
+        shared = (gate / (1.0 + jnp.exp(-gate)) * raised * switch).astype(jnp.bfloat16)
+
+        def term(col):
+            lanes = cols(col, PART)
+            return mm(act, ed_ref[:, lanes]) + mm(shared, sh_buf[2, :, lanes])
+
+        send1[k, 0] = term(core_peer).astype(jnp.bfloat16)
+        send1[k, 1] = term(far_peer).astype(jnp.bfloat16)
+        copy1(k).start()
+        keep_b[k] = term(x_peer)
+        keep_a[k] = term(c)
+
+    def step(s, carry):
+        @pl.when(s < ROWS)
+        def _():
+            @pl.when(s > 0)
+            def _():
+                row_copy(s, down(s)).wait_recv()
+
+            side_copy(s, c, s_core, r_core, core_peer).start()
+            side_copy(s, c, s_x, r_x, x_peer).start()
+
+        @pl.when((s >= 1) & (s < ROWS + 1))
+        def _():
+            side_copy(s - 1, x_peer, s_x, r_x, x_peer).wait_recv()
+            side_copy(s - 1, x_peer, s_fwd, r_fwd, core_peer).start()
+
+        @pl.when((s >= 2) & (s < ROWS + 2))
+        def _():
+            side_copy(s - 2, core_peer, s_core, r_core, core_peer).wait_recv()
+            side_copy(s - 2, far_peer, s_fwd, r_fwd, core_peer).wait_recv()
+            experts(s - 2)
+
+        @pl.when((s >= 3) & (s < ROWS + 3))
+        def _():
+            k = s - 3
+            copy1(k).wait_recv()
+            send2[k] = (keep_b[k] + recv1[k, 1].astype(jnp.float32)).astype(jnp.bfloat16)
+            copy2(k).start()
+            keep_a[k] = keep_a[k] + recv1[k, 0].astype(jnp.float32)
+
+        @pl.when(s >= 4)
+        def _():
+            k = s - 4
+            copy2(k).wait_recv()
+            done = keep_a[k] + recv2[k].astype(jnp.float32)
+            keep_a[k] = done
+
+            @pl.when(k > 0)
+            def _():
+                send3[k] = done.astype(jnp.bfloat16)
+                copy3(k).start()
+
+        return carry
+
+    lax.fori_loop(0, ROWS + 4, step, 0)
+
+    total = own_hidden[...].astype(jnp.float32) + keep_a[0]
+    for k in range(1, ROWS):
+        copy3(k).wait_recv()
+        total = total + recv3[k].astype(jnp.float32)
+    out_ref[...] = total.astype(jnp.bfloat16)
+
+    for k in range(1, REACH + 1):
+
+        @pl.when(r + k < ROWS)
+        def _():
+            k_copy(k).wait_send()
+            v_copy(k).wait_send()
+
+    for k in range(1, COLS):
+        gain_copy(k, c).wait_send()
+        head_copy(k).wait_send()
+    for k in range(ROWS):
+        if k > 0:
+            wo_copy(k, r).wait_send()
+            w_copy(k).wait_send()
+            sh_copy(k, r).wait_send()
+            row_copy(k, r).wait_send()
+            copy3(k).wait_send()
+        side_copy(k, c, s_core, r_core, core_peer).wait_send()
+        side_copy(k, c, s_x, r_x, x_peer).wait_send()
+        side_copy(k, x_peer, s_fwd, r_fwd, core_peer).wait_send()
+        copy1(k).wait_send()
+        copy2(k).wait_send()
+
+
+def fused_body(
+    queries,
+    key_vectors,
+    values,
+    sink_logit,
+    lengths,
+    stream,
+    out_weight,
+    norm_gain,
+    shared_gate,
+    shared_up,
+    shared_down,
+    shared_switch,
+    expert_gate,
+    expert_up,
+    expert_down,
+    routes,
+    route_weights,
+):
+    my_row = lax.axis_index("row")
+    positions = my_row * TOK + jnp.arange(TOK, dtype=jnp.int32)
+    lower = lower_bounds(lengths, positions)[:, None]
+    sink = jnp.broadcast_to(jnp.repeat(sink_logit, HDIM)[None, :], (8, 2 * HDIM))
+    gain = jnp.broadcast_to(norm_gain.astype(jnp.float32)[None, :], (8, PART))
+    units = shared_gate.shape[1] // ROWS
+    shared = jnp.stack(
+        [
+            shared_gate.T.reshape(ROWS, units, SLICE),
+            shared_up.T.reshape(ROWS, units, SLICE),
+            shared_down.reshape(ROWS, units, SLICE),
+        ],
+        1,
+    )
+    shared = jnp.pad(shared, ((0, 0), (0, 0), (0, UNITS - units), (0, 0)))
+    expert_ids = jnp.arange(ROWS, dtype=jnp.int32)
+    token_weights = jnp.sum(
+        jnp.where(routes[None, :, :] == expert_ids[:, None, None], route_weights[None], 0.0), axis=2
+    )
+    token_weights = jnp.broadcast_to(token_weights[:, None, :], (ROWS, 8, TOK))
+    bf16, f32 = jnp.bfloat16, jnp.float32
+    eight = pltpu.SemaphoreType.DMA((ROWS,))
+    four = pltpu.SemaphoreType.DMA((COLS,))
+    pair = pltpu.SemaphoreType.DMA((2, ROWS))
+    vmem = pl.BlockSpec(memory_space=pltpu.VMEM)
+    return pl.pallas_call(
+        layer_kernel,
+        out_shape=(
+            jax.ShapeDtypeStruct(queries.shape, bf16),
+            jax.ShapeDtypeStruct(stream.shape, bf16),
+        ),
+        in_specs=[vmem] * 14,
+        out_specs=(vmem, vmem),
+        scratch_shapes=[
+            pltpu.VMEM((2, (REACH + 1) * TOK, 2 * HDIM), bf16),
+            pltpu.VMEM((2 * HDIM, WIDTH), bf16),
+            pltpu.VMEM((8, WIDTH), f32),
+            pltpu.VMEM((3, UNITS, WIDTH), bf16),
+            pltpu.VMEM((ROWS, 8, TOK), f32),
+            pltpu.VMEM((COLS, TOK, PART), bf16),
+            pltpu.VMEM((COLS, TOK, PART), bf16),
+            pltpu.VMEM((ROWS * TOK, WIDTH), bf16),
+            pltpu.VMEM((TOK, PART), bf16),
+            pltpu.VMEM((ROWS, TOK, PART), f32),
+            pltpu.VMEM((ROWS, TOK, PART), f32),
+            pltpu.VMEM((ROWS, 2, TOK, PART), bf16),
+            pltpu.VMEM((ROWS, 2, TOK, PART), bf16),
+            pltpu.VMEM((ROWS, TOK, PART), bf16),
+            pltpu.VMEM((ROWS, TOK, PART), bf16),
+            pltpu.VMEM((ROWS, TOK, PART), bf16),
+            pltpu.VMEM((ROWS, TOK, PART), bf16),
+            pair,
+            pair,
+            eight,
+            eight,
+            four,
+            four,
+            eight,
+            eight,
+            eight,
+            eight,
+            four,
+            four,
+        ]
+        + [eight] * 14,
+        compiler_params=pltpu.CompilerParams(
+            collective_id=0, has_side_effects=True, vmem_limit_bytes=50 << 20
+        ),
+    )(
+        queries,
+        key_vectors,
+        values,
+        sink,
+        lower,
+        stream,
+        out_weight,
+        gain,
+        shared,
+        shared_switch[None, :],
+        expert_gate[0],
+        expert_up[0],
+        expert_down[0],
+        token_weights,
+    )
+
+
+def gathered_body(
     queries,
     key_vectors,
     values,
@@ -160,8 +614,9 @@
 
 
 def solution(mesh):
+    small = mesh.shape["row"] == ROWS and mesh.shape["col"] == COLS
     return jax.shard_map(
-        body,
+        fused_body if small else gathered_body,
         mesh=mesh,
         in_specs=(
             P("row", "col"),

time: 431 us -> 159 us (0.37)
  waiting for transfers between devices: 330 us -> 0 us
  Pallas kernels: 0 us -> 147 us
  matrix products: 27.7 us -> 0 us
  local copies, waits for them, and re-layouts: 26.9 us -> 7.17 us
  between operations: 14.4 us -> 0.73 us
  blocking collectives: 13.1 us -> 0 us
  starting transfers between devices: 10.6 us -> 0 us
    all_to_all x2 -> x0, waiting for transfers between devices: 187 us -> none  [the longest x1 94.2 us: body(): lax.all_to_all(outgoing, 'row', split_axis=0, concat_axis=0, tiled=True)]
    pallas_call x0 -> x1, Pallas kernels: none -> 147 us  [fused_body(): pl.pallas_call(layer_kernel, out_shape=(jax.ShapeDtypeStruct(queries.shap...]
    all_gather x5 -> x0, waiting for transfers between devices: 106 us -> none  [the longest x1 40.4 us: body(): key_piece = lax.all_gather(key_value, 'row', axis=1, tiled=True)]
    reduce_scatter x2 -> x0, waiting for transfers between devices: 34.8 us -> none  [the longest x1 19.3 us: body(): lax.psum_scatter(layer_terms.astype(jnp.bfloat16), 'col', scatter_dimensi...]
    dot_general x8 -> x0, matrix products: 27.7 us -> none  [the longest x1 8.09 us: body(): jnp.dot(shared_act, lax.all_gather(shared_down, 'row', axis=1, tiled=True...]
    gather x2 -> x0, local copies, waits for them, and re-layouts: 11.8 us -> none  [the longest x1 7.52 us: body(): returned.reshape(row_count * capacity, model_width)[target]]
    all_to_all x2 -> x0, starting transfers between devices: 10.1 us -> none  [the longest x1 5.54 us: body(): lax.all_to_all(outgoing, 'row', split_axis=0, concat_axis=0, tiled=True)]
    all_gather x1 -> x0, blocking collectives: 7.34 us -> none  [body(): normed = lax.all_gather(normed_part, 'col', axis=1, tiled=True)]
  transfers between devices with their start and end apart: 9 -> 0, of which waited for: 7 -> 0; matrix products, arithmetic and copies ran while one was open for 11% -> 0% of each run, Pallas kernels for 0% -> 0%
where the time goes in v1:
time: 159 us
  Pallas kernels  147 us (92%)
  local copies, waits for them, and re-layouts  7.17 us (5%)
  other arithmetic  3.75 us (2%)
    pallas_call x1, Pallas kernels, fused_body(): pl.pallas_call(layer_kernel, out_shape=(jax.ShapeDtypeStruct(queries.shap...  147 us
    unnamed x20, local copies, waits for them, and re-layouts  5.62 us

profile of v1, /device:TPU:0, one launch (start us, length us, event | category | flops | bytes accessed | tf_op | source)
XLA Modules:
  0.0 158.7 jit_solution(13263985466131806960)
XLA Ops:
  0.6 0.0 copy-start
  0.6 0.0 copy-start.7
  0.7 0.9 reduce-window.9
  1.6 0.7 bitcast_subtract_fusion
  2.3 0.1 select_reduce_fusion.1
  2.4 0.0 copy-done
  2.4 0.1 broadcast_bitcast_fusion
  2.4 0.7 select_reduce_fusion
  3.1 0.7 broadcast_in_dim.59.switch_ref
  3.8 0.7 broadcast_in_dim.58.gain_ref
  4.5 0.1 copy.28
  4.6 1.3 fusion.4.sh_ref
  6.0 0.0 copy-done.7
  6.0 1.6 copy.29
  7.6 0.0 copy-start.1
  7.6 0.0 copy-start.2
  7.6 0.0 copy-start.3
  7.6 0.0 copy-start.4
  7.6 0.0 copy-start.5
  7.6 0.0 copy-start.6
  7.6 2.7 %copy.30 = bf16[1,2048,352]{2,1,0:T(8,128)(2,1)} copy(bf16[1,2048,352]{1,2,0:T(8,128)(2,1)} %param.30) | data formatting | bytes 2883584 | tf_op args[13]
  10.3 0.0 copy-done.1
  10.3 0.0 copy-done.2
  10.3 0.0 copy-done.3
  10.3 0.0 copy-done.4
  10.3 0.0 copy-done.5
  10.3 0.0 copy-done.6
  10.4 147.0 %shard_map.176 = (bf16[128,256]{1,0:T(8,128)(2,1)S(1)}, bf16[128,512]{1,0:T(8,128)(2,1)S(1)}) custom-call(bf16[128,256]{1,0:T(8,128)(2,1)S(1)} %copy-done.4, bf16[128,256]{1,0:T(8,128)(2,1)S(1)} %copy-done.5, bf16[128,256]{1,0:T(8,128)(2,1)S(1)} %copy-done.6, f32[8,256]{1,0:T(8,128)S(1)} %broadcast_in_dim.56.sink_ref, ...), custom_call_target="tpu_custom_call" | custom-call | tf_op jit(solution)/shard_map/pallas_call | solution.py:417
  157.4 0.6 copy.33
  158.0 0.7 copy.34
  (4 shorter events, 0.0 us)
Async XLA Ops:
  0.6 1.7 %copy-start = (f32[2]{0:T(128)S(1)}, f32[2]{0:T(128)}, u32[]{:S(2)}) copy-start(f32[2]{0:T(128)} %param.20) | copy-start | bytes 28
  0.6 5.3 %copy-start.7 = (bf16[1,2048,352]{1,2,0:T(8,128)(2,1)S(1)}, bf16[1,2048,352]{1,2,0:T(8,128)(2,1)}, u32[]{:S(2)}) copy-start(bf16[1,2048,352]{1,2,0:T(8,128)(2,1)} %param.29) | copy-start | bytes 4325380
  7.6 2.7 %copy-start.1 = (bf16[1,352,2048]{2,1,0:T(8,128)(2,1)S(1)}, bf16[1,352,2048]{2,1,0:T(8,128)(2,1)}, u32[]{:S(2)}) copy-start(bf16[1,352,2048]{2,1,0:T(8,128)(2,1)} %param.31) | copy-start | bytes 4325380
  7.6 2.7 %copy-start.2 = (bf16[128,512]{1,0:T(8,128)(2,1)S(1)}, bf16[128,512]{1,0:T(8,128)(2,1)}, u32[]{:S(2)}) copy-start(bf16[128,512]{1,0:T(8,128)(2,1)} %stream_ref.1) | copy-start | bytes 393220
  7.6 2.7 %copy-start.3 = (bf16[256,256]{1,0:T(8,128)(2,1)S(1)}, bf16[256,256]{1,0:T(8,128)(2,1)}, u32[]{:S(2)}) copy-start(bf16[256,256]{1,0:T(8,128)(2,1)} %wo_ref.1) | copy-start | bytes 393220
  7.6 2.7 %copy-start.4 = (bf16[128,256]{1,0:T(8,128)(2,1)S(1)}, bf16[128,256]{1,0:T(8,128)(2,1)}, u32[]{:S(2)}) copy-start(bf16[128,256]{1,0:T(8,128)(2,1)} %q_ref.1) | copy-start | bytes 196612
  7.6 2.8 %copy-start.5 = (bf16[128,256]{1,0:T(8,128)(2,1)S(1)}, bf16[128,256]{1,0:T(8,128)(2,1)}, u32[]{:S(2)}) copy-start(bf16[128,256]{1,0:T(8,128)(2,1)} %k_ref.1) | copy-start | bytes 196612
  7.6 2.7 %copy-start.6 = (bf16[128,256]{1,0:T(8,128)(2,1)S(1)}, bf16[128,256]{1,0:T(8,128)(2,1)}, u32[]{:S(2)}) copy-start(bf16[128,256]{1,0:T(8,128)(2,1)} %v_ref.1) | copy-start | bytes 196612

commit v2 on v1

--- a/solution.py
+++ b/solution.py
@@ -33,6 +33,7 @@
 SLICE = WIDTH // ROWS
 UNITS = 96
 REACH = (LONGEST - 2 + TOK) // TOK
+HOPS = REACH // 2
 NT = (((1,), (1,)), ((), ()))
 
 
@@ -45,18 +46,25 @@
     k_ref,
     v_ref,
     sink_ref,
-    lower_ref,
+    lengths_ref,
     stream_ref,
     wo_ref,
     gain_ref,
     sh_ref,
     switch_ref,
+    eg_hbm,
+    eu_hbm,
+    ed_hbm,
+    routes_ref,
+    route_weights_ref,
+    att_ref,
+    out_ref,
     eg_ref,
     eu_ref,
     ed_ref,
-    w_ref,
-    att_ref,
-    out_ref,
+    gain_send,
+    switch_buf,
+    w_send,
     kv_buf,
     wo_buf,
     gain_buf,
@@ -74,6 +82,9 @@
     recv2,
     send3,
     recv3,
+    send4,
+    recv4,
+    s_local,
     s_kv,
     r_kv,
     s_wo,
@@ -88,6 +99,7 @@
     r_head,
     s_row,
     r_row,
+    s_pass,
     s_core,
     r_core,
     s_x,
@@ -100,12 +112,24 @@
     r_2,
     s_3,
     r_3,
+    s_4,
+    r_4,
 ):
     r = lax.axis_index("row")
     c = lax.axis_index("col")
     core_peer = c + 1 - 2 * (c % 2)
     x_peer = (c + 2) % COLS
     far_peer = (core_peer + 2) % COLS
+    depth = ROWS // 2
+    z = r // 2
+    y = r % 2
+    partner = r + 1 - 2 * y
+
+    def ahead(d):
+        return ((z + d) % depth) * 2 + y
+
+    def origin(t):
+        return ((z + depth - t // 2) % depth) * 2 + (y + t % 2) % 2
 
     def up(k):
         return (r + k) % ROWS
@@ -115,6 +139,13 @@
 
     def cols(i, n):
         return pl.ds(pl.multiple_of(i * n, n), n)
+
+    locals_ = [
+        pltpu.make_async_copy(a, b, s_local.at[i])
+        for i, (a, b) in enumerate(((eg_hbm, eg_ref), (eu_hbm, eu_ref), (ed_hbm, ed_ref)))
+    ]
+    for copy in locals_:
+        copy.start()
 
     barrier = pltpu.get_barrier_semaphore()
     for k in range(1, ROWS):
@@ -133,18 +164,22 @@
             device_id_type=MESH,
         )
 
-    def k_copy(k):
-        return push(
-            k_ref, kv_buf.at[0, pl.ds(k * TOK, TOK)], s_kv.at[0, k], r_kv.at[0, k], (up(k), c)
-        )
-
-    def v_copy(k):
-        return push(
-            v_ref, kv_buf.at[1, pl.ds(k * TOK, TOK)], s_kv.at[1, k], r_kv.at[1, k], (up(k), c)
-        )
-
-    def wo_copy(k, block):
-        return push(wo_ref, wo_buf.at[:, cols(block, SLICE)], s_wo.at[k], r_wo.at[k], (up(k), c))
+    def kv_copy(i, from_slot, to_slot, sem, row):
+        own = (k_ref, v_ref)[i]
+        src = own if from_slot == 0 else kv_buf.at[i, pl.ds(from_slot * TOK, TOK)]
+        dst = kv_buf.at[i, cols(to_slot, TOK)]
+        return push(src, dst, s_kv.at[i, sem], r_kv.at[i, to_slot], (row, c))
+
+    def wo_copy(t, sem, row):
+        piece = wo_buf.at[:, cols(origin(t), SLICE)]
+        return push(piece, piece, s_wo.at[sem], r_wo.at[t], (row, c))
+
+    def wo_send(sem, t, row):
+        return push(wo_ref, wo_buf.at[:, cols(r, SLICE)], s_wo.at[sem], r_wo.at[t], (row, c))
+
+    def wo_pass(d):
+        piece = wo_buf.at[:, cols(origin(2 * d), SLICE)]
+        return push(piece, piece, s_wo.at[depth + d], r_wo.at[2 * d + 1], (partner, c))
 
     def sh_copy(k, block):
         return push(
@@ -156,11 +191,11 @@
         )
 
     def w_copy(k):
-        return push(w_ref.at[up(k)], w_buf.at[k], s_w.at[k], r_w.at[k], (up(k), c))
+        return push(w_send.at[up(k)], w_buf.at[k], s_w.at[k], r_w.at[k], (up(k), c))
 
     def gain_copy(k, block):
         return push(
-            gain_ref,
+            gain_send,
             gain_buf.at[:, cols(block, PART)],
             s_gain.at[k],
             r_gain.at[k],
@@ -172,60 +207,112 @@
             head_send.at[k], head_recv.at[k], s_head.at[k], r_head.at[k], (r, (c + k) % COLS)
         )
 
-    for k in range(1, REACH + 1):
-
-        @pl.when(r + k < ROWS)
-        def _():
-            k_copy(k).start()
-            v_copy(k).start()
-
-    for k in range(1, ROWS):
-        wo_copy(k, r).start()
+    def both(fn, *args):
+        for i in range(2):
+            getattr(kv_copy(i, *args), fn)()
+
+    near = 2 * HOPS
+
+    def sends(fn):
+        for d in range(1, HOPS + 1):
+
+            @pl.when(z + d < depth)
+            def _():
+                both(fn, 0, 2 * d, d, jnp.minimum(r + 2 * d, ROWS - 1))
+
+        @pl.when(y == 0)
+        def _():
+            both(fn, 0, 1, 0, partner)
+
+        @pl.when(r == 1)
+        def _():
+            both(fn, 0, REACH, near + 1, r + REACH)
+
+    def handovers(fn):
+        for d in range(1, HOPS + 1):
+
+            @pl.when(z >= d)
+            def _():
+                both(fn, 2 * d, 2 * d + 1 - 2 * y, HOPS + d, partner)
+
+    def arrived(k):
+        @pl.when(r >= k)
+        def _():
+            both("wait_recv", 0, k, 0, partner)
+
+    sends("start")
+    for d in range(1, depth):
+        wo_send(d, 2 * d, ahead(d)).start()
+    wo_send(depth, 1, partner).start()
+
+    for i in range(PART // HDIM):
+        gain_send[:, i * HDIM : (i + 1) * HDIM] = jnp.broadcast_to(
+            gain_ref[i : i + 1, :].astype(jnp.float32), (8, HDIM)
+        )
+    for e in range(ROWS):
+        picked = jnp.where(routes_ref[...] == e, route_weights_ref[...], 0.0)
+        w_send[e] = jnp.broadcast_to(jnp.sum(picked, axis=0, keepdims=True), (8, TOK))
     for k in range(1, COLS):
         gain_copy(k, c).start()
     for k in range(1, ROWS):
         w_copy(k).start()
-    for k in range(1, ROWS):
-        sh_copy(k, r).start()
 
     kv_buf[0, 0:TOK] = k_ref[...]
     kv_buf[1, 0:TOK] = v_ref[...]
     wo_buf[:, cols(r, SLICE)] = wo_ref[...]
-    gain_buf[:, cols(c, PART)] = gain_ref[...]
+    gain_buf[:, cols(c, PART)] = gain_send[...]
     sh_buf[:, :, cols(r, SLICE)] = sh_ref[r]
-    w_buf[0] = w_ref[r]
+    w_buf[0] = w_send[r]
+    for i in range(WIDTH // HDIM):
+        switch_buf[:, i * HDIM : (i + 1) * HDIM] = jnp.broadcast_to(
+            switch_ref[i : i + 1, :].astype(jnp.float32), (8, HDIM)
+        )
 
     for k in range(1, REACH + 1):
 
-        @pl.when(r >= k)
-        def _():
-            k_copy(k).wait_recv()
-            v_copy(k).wait_recv()
-
         @pl.when(r < k)
         def _():
             kv_buf[:, k * TOK : (k + 1) * TOK] = jnp.zeros((2, TOK, 2 * HDIM), jnp.bfloat16)
+
+    for d in range(1, HOPS + 1):
+        arrived(2 * d)
+    handovers("start")
+    for d in range(1, depth - 1):
+        wo_copy(2 * d, 0, partner).wait_recv()
+        wo_pass(d).start()
+    for k in range(1, REACH + 1, 2):
+        arrived(k)
 
     keys = (REACH + 1) * TOK
     place = lax.broadcasted_iota(jnp.int32, (TOK, keys), 1)
     key_place = (r - place // TOK) * TOK + place % TOK
-    positions = r * TOK + lax.broadcasted_iota(jnp.int32, (TOK, keys), 0)
-    visible = (key_place >= lower_ref[...]) & (key_place <= positions)
+    rows_at = r * TOK + lax.broadcasted_iota(jnp.int32, (TOK, 1), 0)
+    lower = jnp.maximum(rows_at - WINDOW + 1, 0)
+    begin = jnp.int32(0)
+    for d in range(lengths_ref.shape[0]):
+        lower = jnp.maximum(lower, jnp.where(rows_at >= begin, begin, 0))
+        begin = begin + lengths_ref[d]
+    visible = (key_place >= lower) & (key_place <= rows_at)
     for h in range(2):
         lanes = slice(h * HDIM, (h + 1) * HDIM)
         scores = lax.dot_general(
             q_ref[:, lanes], kv_buf[0, :, lanes], NT, preferred_element_type=jnp.float32
         ) * (1.0 / math.sqrt(HDIM))
         masked = jnp.where(visible, scores, masked_score)
-        sink = sink_ref[0:1, h * HDIM : h * HDIM + 1]
+        sink = sink_ref[h]
         row_max = jnp.maximum(jnp.max(masked, axis=1, keepdims=True), sink)
         weight = jnp.where(visible, jnp.exp(masked - row_max), 0.0)
         denominator = jnp.exp(sink - row_max) + jnp.sum(weight, axis=1, keepdims=True)
         mixture = mm(weight.astype(jnp.bfloat16), kv_buf[1, :, lanes])
         att_ref[:, lanes] = (mixture / denominator).astype(jnp.bfloat16)
-
-    for k in range(1, ROWS):
-        wo_copy(k, down(k)).wait_recv()
+        if h == 0:
+            wo_copy(2 * depth - 2, 0, partner).wait_recv()
+            wo_pass(depth - 1).start()
+            for k in range(1, ROWS):
+                sh_copy(k, r).start()
+
+    for d in range(depth):
+        wo_copy(2 * d + 1, 0, partner).wait_recv()
     attended = att_ref[...]
     for k in range(1, COLS):
         head_send[k] = mm(attended, wo_buf[:, cols((c + k) % COLS, PART)]).astype(jnp.bfloat16)
@@ -238,17 +325,21 @@
     own_hidden[...] = hidden
     hid[cols(r, TOK), cols(c, PART)] = hidden
 
-    def row_copy(k, block):
+    def row_copy(d):
         return push(
             own_hidden,
-            hid.at[cols(block, TOK), cols(c, PART)],
-            s_row.at[k],
-            r_row.at[k],
-            (up(k), c),
+            hid.at[cols(r, TOK), cols(c, PART)],
+            s_row.at[d],
+            r_row.at[2 * d],
+            (ahead(d), c),
         )
 
+    def pass_copy(t, arrival):
+        piece = hid.at[cols(origin(t), TOK), cols(c, PART)]
+        return push(piece, piece, s_pass.at[t], r_row.at[arrival], (partner, c))
+
     def side_copy(k, col, send, recv, peer):
-        piece = hid.at[cols(down(k), TOK), cols(col, PART)]
+        piece = hid.at[cols(origin(k), TOK), cols(col, PART)]
         return push(piece, piece, send.at[k], recv.at[k], (r, peer))
 
     def copy1(k):
@@ -257,29 +348,34 @@
     def copy2(k):
         return push(send2.at[k], recv2.at[k], s_2.at[k], r_2.at[k], (r, x_peer))
 
-    def copy3(k):
-        return push(send3.at[k], recv3.at[k], s_3.at[k], r_3.at[k], (down(k), c))
-
-    for k in range(1, ROWS):
-        row_copy(k, r).start()
+    def copy3(t):
+        return push(send3.at[t], recv3.at[t // 2], s_3.at[t], r_3.at[t // 2], (partner, c))
+
+    def copy4(d):
+        return push(send4.at[d], recv4.at[d], s_4.at[d], r_4.at[d], (origin(2 * d), c))
+
+    for d in range(1, depth):
+        row_copy(d).start()
 
     for k in range(1, ROWS):
         sh_copy(k, down(k)).wait_recv()
         w_copy(k).wait_recv()
     for k in range(1, COLS):
         gain_copy(k, (c + COLS - k) % COLS).wait_recv()
+    for copy in locals_:
+        copy.wait()
 
     def experts(k):
-        widened = hid[cols(down(k), TOK), :].astype(jnp.float32)
+        row = origin(k)
+        widened = hid[cols(row, TOK), :].astype(jnp.float32)
         mean = jnp.mean(widened * widened, axis=1, keepdims=True)
         normed = (widened * lax.rsqrt(mean + norm_eps) * gain_buf[0:1, :]).astype(jnp.bfloat16)
-        logit = jnp.sum(
-            normed.astype(jnp.float32) * switch_ref[...].astype(jnp.float32), axis=1, keepdims=True
-        )
+        logit = jnp.sum(normed.astype(jnp.float32) * switch_buf[0:1, :], axis=1, keepdims=True)
         switch = 1.0 / (1.0 + jnp.exp(-logit))
-        weights = jnp.broadcast_to(w_buf[k, 0:1, :], (TOK, TOK)).T[:, 0:1]
-        gate = mm(normed, eg_ref[...])
-        act = gate / (1.0 + jnp.exp(-gate)) * mm(normed, eu_ref[...])
+        weights = jnp.broadcast_to(w_buf[(r + ROWS - row) % ROWS, 0:1, :], (TOK, TOK)).T[:, 0:1]
+        gate = lax.dot_general(normed, eg_ref[...], NT, preferred_element_type=jnp.float32)
+        raised = lax.dot_general(normed, eu_ref[...], NT, preferred_element_type=jnp.float32)
+        act = gate / (1.0 + jnp.exp(-gate)) * raised
         act = (act * weights).astype(jnp.bfloat16)
         gate = lax.dot_general(normed, sh_buf[0], NT, preferred_element_type=jnp.float32)
         raised = lax.dot_general(normed, sh_buf[1], NT, preferred_element_type=jnp.float32)
@@ -300,7 +396,11 @@
         def _():
             @pl.when(s > 0)
             def _():
-                row_copy(s, down(s)).wait_recv()
+                pass_copy(s, s).wait_recv()
+
+            @pl.when(s % 2 == 0)
+            def _():
+                pass_copy(s, s + 1).start()
 
             side_copy(s, c, s_core, r_core, core_peer).start()
             side_copy(s, c, s_x, r_x, x_peer).start()
@@ -324,44 +424,59 @@
             copy2(k).start()
             keep_a[k] = keep_a[k] + recv1[k, 0].astype(jnp.float32)
 
-        @pl.when(s >= 4)
+        @pl.when((s >= 4) & (s < ROWS + 4))
         def _():
             k = s - 4
             copy2(k).wait_recv()
             done = keep_a[k] + recv2[k].astype(jnp.float32)
             keep_a[k] = done
 
-            @pl.when(k > 0)
+            @pl.when(k % 2 == 1)
             def _():
                 send3[k] = done.astype(jnp.bfloat16)
                 copy3(k).start()
 
+        @pl.when((s >= 6) & (s % 2 == 0))
+        def _():
+            d = (s - 6) // 2
+            copy3(2 * d + 1).wait_recv()
+            done = keep_a[2 * d] + recv3[d].astype(jnp.float32)
+            keep_a[2 * d] = done
+
+            @pl.when(d > 0)
+            def _():
+                send4[d] = done.astype(jnp.bfloat16)
+                copy4(d).start()
+
         return carry
 
-    lax.fori_loop(0, ROWS + 4, step, 0)
+    lax.fori_loop(0, ROWS + 5, step, 0)
 
     total = own_hidden[...].astype(jnp.float32) + keep_a[0]
-    for k in range(1, ROWS):
-        copy3(k).wait_recv()
-        total = total + recv3[k].astype(jnp.float32)
+    for d in range(1, depth):
+        copy4(d).wait_recv()
+        total = total + recv4[d].astype(jnp.float32)
     out_ref[...] = total.astype(jnp.bfloat16)
 
-    for k in range(1, REACH + 1):
-
-        @pl.when(r + k < ROWS)
-        def _():
-            k_copy(k).wait_send()
-            v_copy(k).wait_send()
+    sends("wait_send")
+    handovers("wait_send")
+    for d in range(1, depth):
+        wo_send(d, 2 * d, ahead(d)).wait_send()
+        wo_pass(d).wait_send()
+        row_copy(d).wait_send()
+        copy4(d).wait_send()
+    wo_send(depth, 1, partner).wait_send()
 
     for k in range(1, COLS):
         gain_copy(k, c).wait_send()
         head_copy(k).wait_send()
     for k in range(ROWS):
         if k > 0:
-            wo_copy(k, r).wait_send()
             w_copy(k).wait_send()
             sh_copy(k, r).wait_send()
-            row_copy(k, r).wait_send()
+        if k % 2 == 0:
+            pass_copy(k, k + 1).wait_send()
+        else:
             copy3(k).wait_send()
         side_copy(k, c, s_core, r_core, core_peer).wait_send()
         side_copy(k, c, s_x, r_x, x_peer).wait_send()
@@ -389,11 +504,6 @@
     routes,
     route_weights,
 ):
-    my_row = lax.axis_index("row")
-    positions = my_row * TOK + jnp.arange(TOK, dtype=jnp.int32)
-    lower = lower_bounds(lengths, positions)[:, None]
-    sink = jnp.broadcast_to(jnp.repeat(sink_logit, HDIM)[None, :], (8, 2 * HDIM))
-    gain = jnp.broadcast_to(norm_gain.astype(jnp.float32)[None, :], (8, PART))
     units = shared_gate.shape[1] // ROWS
     shared = jnp.stack(
         [
@@ -404,25 +514,29 @@
         1,
     )
     shared = jnp.pad(shared, ((0, 0), (0, 0), (0, UNITS - units), (0, 0)))
-    expert_ids = jnp.arange(ROWS, dtype=jnp.int32)
-    token_weights = jnp.sum(
-        jnp.where(routes[None, :, :] == expert_ids[:, None, None], route_weights[None], 0.0), axis=2
-    )
-    token_weights = jnp.broadcast_to(token_weights[:, None, :], (ROWS, 8, TOK))
     bf16, f32 = jnp.bfloat16, jnp.float32
     eight = pltpu.SemaphoreType.DMA((ROWS,))
     four = pltpu.SemaphoreType.DMA((COLS,))
     pair = pltpu.SemaphoreType.DMA((2, ROWS))
     vmem = pl.BlockSpec(memory_space=pltpu.VMEM)
+    smem = pl.BlockSpec(memory_space=pltpu.SMEM)
+    hbm = pl.BlockSpec(memory_space=pl.ANY)
+    hidden_units = expert_down.shape[1]
     return pl.pallas_call(
         layer_kernel,
         out_shape=(
             jax.ShapeDtypeStruct(queries.shape, bf16),
             jax.ShapeDtypeStruct(stream.shape, bf16),
         ),
-        in_specs=[vmem] * 14,
+        in_specs=[vmem] * 3 + [smem] * 2 + [vmem] * 5 + [hbm] * 3 + [vmem] * 2,
         out_specs=(vmem, vmem),
         scratch_shapes=[
+            pltpu.VMEM((hidden_units, WIDTH), bf16),
+            pltpu.VMEM((hidden_units, WIDTH), bf16),
+            pltpu.VMEM((hidden_units, WIDTH), bf16),
+            pltpu.VMEM((8, PART), f32),
+            pltpu.VMEM((8, WIDTH), f32),
+            pltpu.VMEM((ROWS, 8, TOK), f32),
             pltpu.VMEM((2, (REACH + 1) * TOK, 2 * HDIM), bf16),
             pltpu.VMEM((2 * HDIM, WIDTH), bf16),
             pltpu.VMEM((8, WIDTH), f32),
@@ -439,7 +553,10 @@
             pltpu.VMEM((ROWS, TOK, PART), bf16),
             pltpu.VMEM((ROWS, TOK, PART), bf16),
             pltpu.VMEM((ROWS, TOK, PART), bf16),
-            pltpu.VMEM((ROWS, TOK, PART), bf16),
+            pltpu.VMEM((COLS, TOK, PART), bf16),
+            pltpu.VMEM((COLS, TOK, PART), bf16),
+            pltpu.VMEM((COLS, TOK, PART), bf16),
+            pltpu.SemaphoreType.DMA((3,)),
             pair,
             pair,
             eight,
@@ -453,25 +570,26 @@
             four,
             four,
         ]
-        + [eight] * 14,
+        + [eight] * 17,
         compiler_params=pltpu.CompilerParams(
-            collective_id=0, has_side_effects=True, vmem_limit_bytes=50 << 20
+            collective_id=0, has_side_effects=True, vmem_limit_bytes=58 << 20
         ),
     )(
         queries,
         key_vectors,
         values,
-        sink,
-        lower,
+        sink_logit,
+        lengths,
         stream,
         out_weight,
-        gain,
+        norm_gain.reshape(PART // HDIM, HDIM),
         shared,
-        shared_switch[None, :],
-        expert_gate[0],
-        expert_up[0],
+        shared_switch.reshape(WIDTH // HDIM, HDIM),
+        expert_gate[0].T,
+        expert_up[0].T,
         expert_down[0],
-        token_weights,
+        routes.T,
+        route_weights.T,
     )
 
 

time: 159 us -> 132 us (0.83)
  Pallas kernels: 147 us -> 126 us
  local copies, waits for them, and re-layouts: 7.17 us -> 3.04 us
    pallas_call x1, Pallas kernels: 147 us -> 126 us  [fused_body(): pl.pallas_call(layer_kernel, out_shape=(jax.ShapeDtypeStruct(queries.shap...]
    unnamed x20 -> x2, local copies, waits for them, and re-layouts: 5.62 us -> 3.04 us
where the time goes in v2:
time: 132 us
  Pallas kernels  126 us (95%)
  local copies, waits for them, and re-layouts  3.04 us (2%)
  other arithmetic  2.36 us (2%)
    pallas_call x1, Pallas kernels, fused_body(): pl.pallas_call(layer_kernel, out_shape=(jax.ShapeDtypeStruct(queries.shap...  126 us
    unnamed x2, local copies, waits for them, and re-layouts  3.04 us

profile of v2, /device:TPU:0, one launch (start us, length us, event | category | flops | bytes accessed | tf_op | source)
XLA Modules:
  0.0 132.1 jit_solution(4219148877437675115)
XLA Ops:
  0.6 2.4 %fusion.4.sh_ref = bf16[8,3,96,256]{3,2,1,0:T(8,128)(2,1)} fusion(bf16[8,1,88,256]{3,2,1,0:T(8,128)(2,1)} %bitcast.21, bf16[8,1,88,256]{3,2,1,0:T(8,128)(2,1)} %bitcast.22, bf16[8,1,88,256]{3,2,1,0:T(8,128)(2,1)} %bitcast.23), kind=kLoop, calls=%fused_computation.5 | loop fusion | flops 5898240 | bytes 2260992 | tf_op jit(solution)/shard_map/stack | solution.py:508
  3.0 126.1 %shard_map.176 = (bf16[128,256]{1,0:T(8,128)(2,1)}, bf16[128,512]{1,0:T(8,128)(2,1)}) custom-call(bf16[128,256]{1,0:T(8,128)(2,1)} %q_ref.1, bf16[128,256]{1,0:T(8,128)(2,1)} %k_ref.1, bf16[128,256]{1,0:T(8,128)(2,1)} %v_ref.1, f32[2]{0:T(128)} %sink_ref.1, s32[8]{0:T(128)} %lengths_ref.1, bf16[128,512]{1,0:T(8,128)(2,1)} %stream_ref.1, ...), custom_call_target="tpu_custom_call" | custom-call | tf_op jit(solution)/shard_map/pallas_call | solution.py:525
  129.1 1.5 %copy.21 = bf16[128,256]{1,0:T(8,128)(2,1)} copy(bf16[128,256]{1,0:T(8,128)(2,1)} %get-tuple-element.4) | data formatting | bytes 131072
  130.6 1.6 %copy.22 = bf16[128,512]{1,0:T(8,128)(2,1)} copy(bf16[128,512]{1,0:T(8,128)(2,1)} %get-tuple-element.5) | data formatting | bytes 262144

commit v3 on v2

--- a/solution.py
+++ b/solution.py
@@ -59,16 +59,13 @@
     route_weights_ref,
     att_ref,
     out_ref,
-    eg_ref,
-    eu_ref,
-    ed_ref,
+    weights,
     gain_send,
     switch_buf,
     w_send,
     kv_buf,
     wo_buf,
     gain_buf,
-    sh_buf,
     w_buf,
     head_send,
     head_recv,
@@ -140,9 +137,12 @@
     def cols(i, n):
         return pl.ds(pl.multiple_of(i * n, n), n)
 
+    routed_units = eg_hbm.shape[0]
+    own_units = weights.at[:, 0:routed_units]
+    sh_buf = weights.at[:, routed_units : routed_units + UNITS]
     locals_ = [
         pltpu.make_async_copy(a, b, s_local.at[i])
-        for i, (a, b) in enumerate(((eg_hbm, eg_ref), (eu_hbm, eu_ref), (ed_hbm, ed_ref)))
+        for i, (a, b) in enumerate(((eg_hbm, own_units.at[0]), (eu_hbm, own_units.at[1]), (ed_hbm, own_units.at[2])))
     ]
     for copy in locals_:
         copy.start()
@@ -342,6 +342,10 @@
         piece = hid.at[cols(origin(k), TOK), cols(col, PART)]
         return push(piece, piece, send.at[k], recv.at[k], (r, peer))
 
+    def cross_pass(t):
+        piece = hid.at[cols(origin(t), TOK), cols(x_peer, PART)]
+        return push(piece, piece, s_x.at[t + 1], r_x.at[t + 1], (partner, c))
+
     def copy1(k):
         return push(send1.at[k], recv1.at[k], s_1.at[k], r_1.at[k], (r, core_peer))
 
@@ -357,13 +361,14 @@
     for d in range(1, depth):
         row_copy(d).start()
 
-    for k in range(1, ROWS):
-        sh_copy(k, down(k)).wait_recv()
-        w_copy(k).wait_recv()
-    for k in range(1, COLS):
-        gain_copy(k, (c + COLS - k) % COLS).wait_recv()
-    for copy in locals_:
-        copy.wait()
+    def ready():
+        for k in range(1, ROWS):
+            sh_copy(k, down(k)).wait_recv()
+            w_copy(k).wait_recv()
+        for k in range(1, COLS):
+            gain_copy(k, (c + COLS - k) % COLS).wait_recv()
+        for copy in locals_:
+            copy.wait()
 
     def experts(k):
         row = origin(k)
@@ -372,18 +377,16 @@
         normed = (widened * lax.rsqrt(mean + norm_eps) * gain_buf[0:1, :]).astype(jnp.bfloat16)
         logit = jnp.sum(normed.astype(jnp.float32) * switch_buf[0:1, :], axis=1, keepdims=True)
         switch = 1.0 / (1.0 + jnp.exp(-logit))
-        weights = jnp.broadcast_to(w_buf[(r + ROWS - row) % ROWS, 0:1, :], (TOK, TOK)).T[:, 0:1]
-        gate = lax.dot_general(normed, eg_ref[...], NT, preferred_element_type=jnp.float32)
-        raised = lax.dot_general(normed, eu_ref[...], NT, preferred_element_type=jnp.float32)
-        act = gate / (1.0 + jnp.exp(-gate)) * raised
-        act = (act * weights).astype(jnp.bfloat16)
-        gate = lax.dot_general(normed, sh_buf[0], NT, preferred_element_type=jnp.float32)
-        raised = lax.dot_general(normed, sh_buf[1], NT, preferred_element_type=jnp.float32)
-        shared = (gate / (1.0 + jnp.exp(-gate)) * raised * switch).astype(jnp.bfloat16)
+        share = jnp.broadcast_to(w_buf[(r + ROWS - row) % ROWS, 0:1, :], (TOK, TOK)).T[:, 0:1]
+        gate = lax.dot_general(normed, weights[0], NT, preferred_element_type=jnp.float32)
+        raised = lax.dot_general(normed, weights[1], NT, preferred_element_type=jnp.float32)
+        unit = lax.broadcasted_iota(jnp.int32, gate.shape, 1)
+        act = gate / (1.0 + jnp.exp(-gate)) * raised * jnp.where(unit < routed_units, share, switch)
+        act = act.astype(jnp.bfloat16)
 
         def term(col):
             lanes = cols(col, PART)
-            return mm(act, ed_ref[:, lanes]) + mm(shared, sh_buf[2, :, lanes])
+            return mm(act, weights[2, :, lanes])
 
         send1[k, 0] = term(core_peer).astype(jnp.bfloat16)
         send1[k, 1] = term(far_peer).astype(jnp.bfloat16)
@@ -401,32 +404,42 @@
             @pl.when(s % 2 == 0)
             def _():
                 pass_copy(s, s + 1).start()
+                side_copy(s, c, s_x, r_x, x_peer).start()
 
             side_copy(s, c, s_core, r_core, core_peer).start()
-            side_copy(s, c, s_x, r_x, x_peer).start()
 
         @pl.when((s >= 1) & (s < ROWS + 1))
         def _():
             side_copy(s - 1, x_peer, s_x, r_x, x_peer).wait_recv()
+
+            @pl.when(s % 2 == 1)
+            def _():
+                cross_pass(s - 1).start()
+
             side_copy(s - 1, x_peer, s_fwd, r_fwd, core_peer).start()
 
-        @pl.when((s >= 2) & (s < ROWS + 2))
-        def _():
-            side_copy(s - 2, core_peer, s_core, r_core, core_peer).wait_recv()
-            side_copy(s - 2, far_peer, s_fwd, r_fwd, core_peer).wait_recv()
-            experts(s - 2)
-
-        @pl.when((s >= 3) & (s < ROWS + 3))
-        def _():
-            k = s - 3
+        @pl.when(s == 4)
+        def _():
+            ready()
+
+        @pl.when((s >= 4) & (s < ROWS + 4))
+        def _():
+            k = s - 4
+            side_copy(k, core_peer, s_core, r_core, core_peer).wait_recv()
+            side_copy(k, far_peer, s_fwd, r_fwd, core_peer).wait_recv()
+            experts(k)
+
+        @pl.when((s >= 5) & (s < ROWS + 5))
+        def _():
+            k = s - 5
             copy1(k).wait_recv()
             send2[k] = (keep_b[k] + recv1[k, 1].astype(jnp.float32)).astype(jnp.bfloat16)
             copy2(k).start()
             keep_a[k] = keep_a[k] + recv1[k, 0].astype(jnp.float32)
 
-        @pl.when((s >= 4) & (s < ROWS + 4))
-        def _():
-            k = s - 4
+        @pl.when((s >= 6) & (s < ROWS + 6))
+        def _():
+            k = s - 6
             copy2(k).wait_recv()
             done = keep_a[k] + recv2[k].astype(jnp.float32)
             keep_a[k] = done
@@ -436,9 +449,9 @@
                 send3[k] = done.astype(jnp.bfloat16)
                 copy3(k).start()
 
-        @pl.when((s >= 6) & (s % 2 == 0))
-        def _():
-            d = (s - 6) // 2
+        @pl.when((s >= 8) & (s % 2 == 0))
+        def _():
+            d = (s - 8) // 2
             copy3(2 * d + 1).wait_recv()
             done = keep_a[2 * d] + recv3[d].astype(jnp.float32)
             keep_a[2 * d] = done
@@ -450,7 +463,7 @@
 
         return carry
 
-    lax.fori_loop(0, ROWS + 5, step, 0)
+    lax.fori_loop(0, ROWS + 7, step, 0)
 
     total = own_hidden[...].astype(jnp.float32) + keep_a[0]
     for d in range(1, depth):
@@ -476,10 +489,11 @@
             sh_copy(k, r).wait_send()
         if k % 2 == 0:
             pass_copy(k, k + 1).wait_send()
+            side_copy(k, c, s_x, r_x, x_peer).wait_send()
+            cross_pass(k).wait_send()
         else:
             copy3(k).wait_send()
         side_copy(k, c, s_core, r_core, core_peer).wait_send()
-        side_copy(k, c, s_x, r_x, x_peer).wait_send()
         side_copy(k, x_peer, s_fwd, r_fwd, core_peer).wait_send()
         copy1(k).wait_send()
         copy2(k).wait_send()
@@ -520,7 +534,7 @@
     pair = pltpu.SemaphoreType.DMA((2, ROWS))
     vmem = pl.BlockSpec(memory_space=pltpu.VMEM)
     smem = pl.BlockSpec(memory_space=pltpu.SMEM)
-    hbm = pl.BlockSpec(memory_space=pl.ANY)
+    hbm = pl.BlockSpec(memory_space=pltpu.HBM)
     hidden_units = expert_down.shape[1]
     return pl.pallas_call(
         layer_kernel,
@@ -531,16 +545,13 @@
         in_specs=[vmem] * 3 + [smem] * 2 + [vmem] * 5 + [hbm] * 3 + [vmem] * 2,
         out_specs=(vmem, vmem),
         scratch_shapes=[
-            pltpu.VMEM((hidden_units, WIDTH), bf16),
-            pltpu.VMEM((hidden_units, WIDTH), bf16),
-            pltpu.VMEM((hidden_units, WIDTH), bf16),
+            pltpu.VMEM((3, hidden_units + UNITS, WIDTH), bf16),
             pltpu.VMEM((8, PART), f32),
             pltpu.VMEM((8, WIDTH), f32),
             pltpu.VMEM((ROWS, 8, TOK), f32),
             pltpu.VMEM((2, (REACH + 1) * TOK, 2 * HDIM), bf16),
             pltpu.VMEM((2 * HDIM, WIDTH), bf16),
             pltpu.VMEM((8, WIDTH), f32),
-            pltpu.VMEM((3, UNITS, WIDTH), bf16),
             pltpu.VMEM((ROWS, 8, TOK), f32),
             pltpu.VMEM((COLS, TOK, PART), bf16),
             pltpu.VMEM((COLS, TOK, PART), bf16),
@@ -572,7 +583,7 @@
         ]
         + [eight] * 17,
         compiler_params=pltpu.CompilerParams(
-            collective_id=0, has_side_effects=True, vmem_limit_bytes=58 << 20
+            collective_id=0, has_side_effects=True, vmem_limit_bytes=44 << 20
         ),
     )(
         queries,

time: 132 us -> 126 us (0.955)
  Pallas kernels: 126 us -> 120 us
    pallas_call x1, Pallas kernels: 126 us -> 120 us  [fused_body(): pl.pallas_call(layer_kernel, out_shape=(jax.ShapeDtypeStruct(queries.shap...]
    unnamed x2 -> x30, local copies, waits for them, and re-layouts: 3.04 us -> 4.24 us
where the time goes in v3:
time: 126 us
  Pallas kernels  120 us (95%)
  local copies, waits for them, and re-layouts  4.24 us (3%)
  other arithmetic  1.45 us (1%)
    pallas_call x1, Pallas kernels, fused_body(): pl.pallas_call(layer_kernel, out_shape=(jax.ShapeDtypeStruct(queries.shap...  120 us
    unnamed x30, local copies, waits for them, and re-layouts  4.24 us

profile of v3, /device:TPU:0, one launch (start us, length us, event | category | flops | bytes accessed | tf_op | source)
XLA Modules:
  0.0 126.3 jit_solution(18174107108498205159)
XLA Ops:
  0.6 0.0 copy-start.10
  0.6 0.0 copy-start.9
  0.7 0.0 copy-start
  0.7 0.0 copy-start.8
  0.7 0.0 copy-start.11
  0.7 0.0 copy-start.4
  0.7 0.0 copy-start.3
  0.7 0.0 copy-start.13
  0.7 0.0 copy-start.12
  0.7 0.0 copy-start.7
  0.7 0.0 copy-start.6
  0.7 0.0 copy-start.5
  0.8 1.5 %fusion.4.sh_ref = bf16[8,3,96,256]{3,2,1,0:T(8,128)(2,1)S(1)} fusion(bf16[8,1,88,256]{3,2,1,0:T(8,128)(2,1)} %bitcast.25, bf16[8,1,88,256]{3,2,1,0:T(8,128)(2,1)} %bitcast.26, bf16[8,1,88,256]{3,2,1,0:T(8,128)(2,1)} %bitcast.27), kind=kLoop, calls=%fused_computation.5 | loop fusion | flops 5898240 | bytes 2260992 | tf_op jit(solution)/shard_map/stack | solution.py:522
  2.2 0.0 copy-done.10
  2.2 0.0 copy-done.9
  2.2 0.1 copy-done
  2.4 0.0 copy-done.8
  2.4 0.0 copy-done.11
  2.4 0.0 copy-done.4
  2.4 0.0 copy-done.3
  2.4 0.0 copy-done.13
  2.4 0.0 copy-done.12
  2.4 0.0 copy-done.7
  2.4 0.0 copy-done.6
  2.4 0.0 copy-done.5
  2.4 0.0 copy-start.1
  2.4 1.4 %copy-done.1 = bf16[1,2048,352]{1,2,0:T(8,128)(2,1)S(1)} copy-done((bf16[1,2048,352]{1,2,0:T(8,128)(2,1)S(1)}, bf16[1,2048,352]{1,2,0:T(8,128)(2,1)}, u32[]{:S(2)}) %copy-start.1) | copy-done | bytes 1441816
  3.8 0.0 copy-start.2
  3.8 1.4 %copy-done.2 = bf16[1,352,2048]{2,1,0:T(8,128)(2,1)S(1)} copy-done((bf16[1,352,2048]{2,1,0:T(8,128)(2,1)S(1)}, bf16[1,352,2048]{2,1,0:T(8,128)(2,1)}, u32[]{:S(2)}) %copy-start.2) | copy-done | bytes 1441816
  5.2 119.8 %shard_map.176 = (bf16[128,256]{1,0:T(8,128)(2,1)S(1)}, bf16[128,512]{1,0:T(8,128)(2,1)S(1)}) custom-call(bf16[128,256]{1,0:T(8,128)(2,1)S(1)} %copy-done.5, bf16[128,256]{1,0:T(8,128)(2,1)S(1)} %copy-done.6, bf16[128,256]{1,0:T(8,128)(2,1)S(1)} %copy-done.7, f32[2]{0:T(128)S(1)} %copy-done.12, s32[8]{0:T(128)S(1)} %copy-done.13, ...), custom_call_target="tpu_custom_call" | custom-call | tf_op jit(solution)/shard_map/pallas_call | solution.py:539
  125.0 0.6 copy.21
  125.6 0.7 copy.22
Async XLA Ops:
  0.6 1.6 %copy-start.10 = (f32[128,4]{0,1:T(4,128)S(1)}, f32[128,4]{0,1:T(4,128)}, u32[]{:S(2)}) copy-start(f32[128,4]{0,1:T(4,128)} %param.33) | copy-start | bytes 6148
  0.6 1.6 %copy-start.9 = (s32[128,4]{0,1:T(4,128)S(1)}, s32[128,4]{0,1:T(4,128)}, u32[]{:S(2)}) copy-start(s32[128,4]{0,1:T(4,128)} %param.32) | copy-start | bytes 6148
  0.7 1.7 %copy-start = (bf16[1,2048,352]{1,2,0:T(8,128)(2,1)S(1)}, bf16[1,2048,352]{1,2,0:T(8,128)(2,1)}, u32[]{:S(2)}) copy-start(bf16[1,2048,352]{1,2,0:T(8,128)(2,1)} %param.29) | copy-start | bytes 4325380
  0.7 1.7 %copy-start.8 = (bf16[2048]{0:T(1024)(128)(2,1)S(1)}, bf16[2048]{0:T(1024)(128)(2,1)}, u32[]{:S(2)}) copy-start(bf16[2048]{0:T(1024)(128)(2,1)} %param.28) | copy-start | bytes 12292
  0.7 1.7 %copy-start.11 = (bf16[512]{0:T(512)(128)(2,1)S(1)}, bf16[512]{0:T(512)(128)(2,1)}, u32[]{:S(2)}) copy-start(bf16[512]{0:T(512)(128)(2,1)} %param.24) | copy-start | bytes 3076
  0.7 1.7 %copy-start.4 = (bf16[256,256]{1,0:T(8,128)(2,1)S(1)}, bf16[256,256]{1,0:T(8,128)(2,1)}, u32[]{:S(2)}) copy-start(bf16[256,256]{1,0:T(8,128)(2,1)} %wo_ref.1) | copy-start | bytes 393220
  0.7 1.7 %copy-start.3 = (bf16[128,512]{1,0:T(8,128)(2,1)S(1)}, bf16[128,512]{1,0:T(8,128)(2,1)}, u32[]{:S(2)}) copy-start(bf16[128,512]{1,0:T(8,128)(2,1)} %stream_ref.1) | copy-start | bytes 393220
  0.7 1.7 %copy-start.13 = (s32[8]{0:T(128)S(1)}, s32[8]{0:T(128)}, u32[]{:S(2)}) copy-start(s32[8]{0:T(128)} %lengths_ref.1) | copy-start | bytes 100
  0.7 1.7 %copy-start.12 = (f32[2]{0:T(128)S(1)}, f32[2]{0:T(128)}, u32[]{:S(2)}) copy-start(f32[2]{0:T(128)} %sink_ref.1) | copy-start | bytes 28
  0.7 1.7 %copy-start.7 = (bf16[128,256]{1,0:T(8,128)(2,1)S(1)}, bf16[128,256]{1,0:T(8,128)(2,1)}, u32[]{:S(2)}) copy-start(bf16[128,256]{1,0:T(8,128)(2,1)} %v_ref.1) | copy-start | bytes 196612
  0.7 1.7 %copy-start.6 = (bf16[128,256]{1,0:T(8,128)(2,1)S(1)}, bf16[128,256]{1,0:T(8,128)(2,1)}, u32[]{:S(2)}) copy-start(bf16[128,256]{1,0:T(8,128)(2,1)} %k_ref.1) | copy-start | bytes 196612
  0.7 1.7 %copy-start.5 = (bf16[128,256]{1,0:T(8,128)(2,1)S(1)}, bf16[128,256]{1,0:T(8,128)(2,1)}, u32[]{:S(2)}) copy-start(bf16[128,256]{1,0:T(8,128)(2,1)} %q_ref.1) | copy-start | bytes 196612
  2.4 1.4 %copy-start.1 = (bf16[1,2048,352]{1,2,0:T(8,128)(2,1)S(1)}, bf16[1,2048,352]{1,2,0:T(8,128)(2,1)}, u32[]{:S(2)}) copy-start(bf16[1,2048,352]{1,2,0:T(8,128)(2,1)} %param.30) | copy-start | bytes 4325380
  3.8 1.4 %copy-start.2 = (bf16[1,352,2048]{2,1,0:T(8,128)(2,1)S(1)}, bf16[1,352,2048]{2,1,0:T(8,128)(2,1)}, u32[]{:S(2)}) copy-start(bf16[1,352,2048]{2,1,0:T(8,128)(2,1)} %param.31) | copy-start | bytes 4325380
